TPU v7x, 32 devices: a whole 2x2x4 slice. The times are simulated.
32 devices in a mesh: row: 4 (over z), col: 8 (over y, x, core).
Axes of the slice: x: 2, y: 2, z: 4, core: 2. Of those that a mesh axis runs over, the one named last changes fastest.
Arguments:
- amplitudes: bfloat16 [16, 16, 12, 4096], P('row', 'col'), may hold values from -6 to 6
- integrals: bfloat16 [16, 16, 47, 4096], P('row', 'col'), may hold values from -0.1875 to 0.1875
- pair_lists: int32 [4, 12, 2], replicated, may hold values from 0 to 46, as said below
- tile_counts: int32 [4], replicated, may hold values from 1 to 12, as said below
Outputs:
- symmetric: float32 [16, 16, 12, 4096], P('row', 'col')
Inputs may be any that keep to these rules, and one draw needn't show every extreme that they name: `pair_lists`: each grid row lists 12 distinct ordered pairs of different tiles. `tile_counts`: the largest count equals 12.
All inputs are finite; a program needn't handle non-finite values.
Results may differ from a plain program's by a relative error of at most 0.0029.
Values may be sent and summed in bfloat16 or wider, within the bound.
No kernel may reach another device: no remote copies, remote signals or barrier semaphores. Data moves between devices by JAX's collectives and lax.ppermute only.
A program may use at most 128 MiB of HBM per device.

v0:
```python
import jax
import jax.numpy as jnp
from jax import lax
from jax.sharding import PartitionSpec as P

TILE = 64


def on_device(amplitudes, integrals, pair_lists, tile_counts):
    occ_row, occ_col, slot_count, square = amplitudes.shape
    tile_width = TILE
    row_devices = lax.axis_size("row")
    col_devices = lax.axis_size("col")
    col_ratio = col_devices // row_devices
    my_row = lax.axis_index("row")
    my_col = lax.axis_index("col")
    partner_row = my_col // col_ratio
    tile_first = pair_lists[:, :, 0]
    tile_second = pair_lists[:, :, 1]
    packed = jnp.take(integrals, tile_second.reshape(-1), axis=2)
    packed = packed.reshape(occ_row, occ_col, row_devices, slot_count, square)
    received = lax.all_to_all(packed, "row", split_axis=2, concat_axis=0, tiled=True)
    received = received.reshape(occ_row * row_devices, occ_col, slot_count, square)
    piece = lax.all_gather(amplitudes, "col", axis=1, tiled=True)
    piece_count = piece.shape[1]
    left_tiles = piece.reshape(occ_row, piece_count, slot_count, tile_width, tile_width)
    right_tiles = received.reshape(piece_count, occ_col, slot_count, tile_width, tile_width)
    cycle_sum = jnp.einsum(
        "iksac,kjscb->ijsab", left_tiles, right_tiles, preferred_element_type=jnp.float32
    )
    my_count = lax.dynamic_index_in_dim(tile_counts, my_row, 0, keepdims=False)
    live_slots = (jnp.arange(slot_count, dtype=jnp.int32) < my_count).astype(jnp.float32)
    cycle_value = (cycle_sum * live_slots[None, None, :, None, None]).astype(jnp.bfloat16)
    cycle = cycle_value.reshape(occ_row, occ_col, slot_count, square)
    residual_strip = lax.all_gather(cycle, "row", axis=0, tiled=True)
    mirror_whole = lax.all_to_all(residual_strip, "col", split_axis=0, concat_axis=1, tiled=True)
    mirror_block = lax.dynamic_slice_in_dim(mirror_whole, my_row * occ_row, occ_row, 1)
    mirror_block = mirror_block.reshape(occ_col, occ_row, slot_count, tile_width, tile_width)
    mine_first = lax.dynamic_index_in_dim(tile_first, my_row, 0, keepdims=False)
    mine_second = lax.dynamic_index_in_dim(tile_second, my_row, 0, keepdims=False)
    their_first = lax.dynamic_index_in_dim(tile_first, partner_row, 0, keepdims=False)
    their_second = lax.dynamic_index_in_dim(tile_second, partner_row, 0, keepdims=False)
    pair_match = (
        (mine_first[:, None] == their_second[None, :])
        & (mine_second[:, None] == their_first[None, :])
    ).astype(jnp.bfloat16)
    crossed = jnp.einsum(
        "st,jitba->ijsab", pair_match, mirror_block, preferred_element_type=jnp.float32
    )
    own_part = cycle_value.astype(jnp.float32)
    symmetric = (own_part + crossed) * live_slots[None, None, :, None, None]
    return symmetric.reshape(occ_row, occ_col, slot_count, square)


def solution(mesh):
    return jax.shard_map(
        on_device,
        mesh=mesh,
        in_specs=(P("row", "col", None, None), P("row", "col", None, None), P(), P()),
        out_specs=P("row", "col", None, None),
        check_vma=False,
    )
```

profile of v0, /device:TPU:0, one launch (start us, length us, event | category | flops | bytes accessed | tf_op | source)
XLA Modules:
  0.0 288.4 jit_solution(7167490492308642510)
XLA Ops:
  6.5 0.0 copy-start
  6.5 0.0 all-gather.3.cloned.1.call-start
  6.5 2.8 copy.17
  9.3 0.0 all-gather.3.cloned.1.call-update
  9.3 0.8 fusion.29
  10.1 0.1 reshape_squeeze.6
  10.2 8.5 %gather_fusion = bf16[48,4,2,4096]{3,2,1,0:T(2,128)(2,1)} fusion(bf16[4,2,47,4096]{3,1,2,0:T(2,128)(2,1)S(1)} %copy-done, s32[1024]{0:T(1024)S(1)} %pad_clamp_fusion), kind=kCustom, calls=%fused_computation | custom fusion | bytes 6291648 | tf_op jit(solution)/shard_map/jit(_take)/gather | solution.py:20
  18.8 6.7 %broadcast_select_fusion = bf16[4,2,4,12,4096]{4,1,3,0,2:T(2,128)(2,1)} fusion(pred[4,12]{1,0:T(4,128)(4,1)S(1)} %compare_and_fusion, bf16[4,2,4,12,4096]{4,1,0,3,2:T(2,128)(2,1)} %bitcast.67), kind=kLoop, calls=%fused_computation.4 | loop fusion | flops 1572864 | bytes 6291504 | tf_op jit(solution)/shard_map/jit(_take)/select_n | solution.py:20
  25.4 6.4 %all-to-all-start = ((bf16[4,2,4,12,4096]{4,1,3,0,2:T(2,128)(2,1)}), bf16[4,2,4,12,4096]{4,1,3,0,2:T(2,128)(2,1)}, u32[]{:S(2)}, u32[]{:S(2)}) async-start(bf16[4,2,4,12,4096]{4,1,3,0,2:T(2,128)(2,1)} %broadcast_select_fusion), calls=%async_computation | async-start | bytes 6291456 | tf_op jit(solution)/shard_map/all_to_all | solution.py:22
  31.9 0.0 all-gather.5.cloned.1.call-start
  31.9 0.6 dynamic_slice.20
  32.5 0.6 compare_convert_fusion
  33.1 69.6 %all-to-all-done = bf16[4,2,4,12,4096]{4,1,3,0,2:T(2,128)(2,1)} async-done(((bf16[4,2,4,12,4096]{4,1,3,0,2:T(2,128)(2,1)}), bf16[4,2,4,12,4096]{4,1,3,0,2:T(2,128)(2,1)}, u32[]{:S(2)}, u32[]{:S(2)}) %all-to-all-start) | async-done | bytes 3145760 | tf_op jit(solution)/shard_map/all_to_all | solution.py:22
  102.7 11.1 %reshape_reshape.3 = bf16[16,2,12,64,64]{4,3,1,2,0:T(8,128)(2,1)} reshape(bf16[4,4,2,1,12,4096]{5,2,4,1,0,3:T(2,128)(2,1)} %bitcast.5) | data formatting | bytes 6291456 | tf_op jit(solution)/shard_map/reshape;reshape | solution.py:27
  113.8 9.4 %copy.18 = bf16[4,16,12,4096]{3,1,0,2:T(8,128)(2,1)} copy(bf16[4,16,12,4096]{3,0,2,1:T(4,128)(2,1)} %all-gather.3.cloned.1.call-done) | data formatting | bytes 12582912 | tf_op jit(solution)/shard_map/all_gather | solution.py:24
  123.2 17.9 %reshape.81 = bf16[4,16,12,64,64,1]{4,3,1,0,2,5:T(8,128)(2,1)} reshape(bf16[4,16,12,4096]{3,1,0,2:T(8,128)(2,1)} %copy.18) | data formatting | bytes 12582912 | tf_op jit(solution)/shard_map/reshape | solution.py:26
  141.1 11.1 %fusion.11 = bf16[4,2,12,64,64]{3,4,0,1,2:T(8,128)(2,1)S(1)} fusion(f32[12]{0:T(128)S(1)} %compare_convert_fusion, bf16[4,16,12,64,64,1]{4,3,1,0,2,5:T(8,128)(2,1)} %reshape.81, bf16[16,2,12,64,64]{4,3,1,2,0:T(8,128)(2,1)} %reshape_reshape.3), kind=kOutput, calls=%fused_computation.11 | convolution fusion | flops 806092800 | bytes 10223664 | tf_op jit(solution)/shard_map/iksac,kjscb->ijsab/dot_general | solution.py:28
  152.2 1.7 copy.20
  153.9 3.9 %reshape.69 = bf16[4,2,12,4096]{3,1,2,0:T(2,128)(2,1)} reshape(bf16[4,2,12,64,64]{4,3,1,2,0:T(8,128)(2,1)} %copy.20) | data formatting | bytes 1572864 | tf_op jit(solution)/shard_map/reshape | solution.py:34
  157.7 0.0 all-gather.5.cloned.1.call-update
  157.8 0.0 copy-done.2
  157.8 62.7 %all-gather.5.cloned.1.call-done = bf16[16,2,12,4096]{3,1,2,0:T(2,128)(2,1)} async-done(((bf16[4,2,12,4096]{3,1,2,0:T(2,128)(2,1)}), bf16[16,2,12,4096]{3,1,2,0:T(2,128)(2,1)}) %all-gather.5.cloned.1.call-update) | async-done | bytes 3145744 | tf_op jit(solution)/shard_map/all_gather | solution.py:35
  220.4 4.7 %all-to-all-start.1 = ((bf16[16,2,12,4096]{3,1,2,0:T(2,128)(2,1)}), bf16[16,2,12,4096]{3,1,2,0:T(2,128)(2,1)}, u32[]{:S(2)}, u32[]{:S(2)}) async-start(bf16[16,2,12,4096]{3,1,2,0:T(2,128)(2,1)} %all-gather.5.cloned.1.call-done), calls=%async_computation.1 | async-start | bytes 6291456 | tf_op jit(solution)/shard_map/all_to_all | solution.py:36
  225.2 37.6 %all-to-all-done.1 = bf16[16,2,12,4096]{3,1,2,0:T(2,128)(2,1)} async-done(((bf16[16,2,12,4096]{3,1,2,0:T(2,128)(2,1)}), bf16[16,2,12,4096]{3,1,2,0:T(2,128)(2,1)}, u32[]{:S(2)}, u32[]{:S(2)}) %all-to-all-start.1) | async-done | bytes 3145760 | tf_op jit(solution)/shard_map/all_to_all | solution.py:36
  262.8 5.1 %copy.21 = bf16[8,2,2,12,4096]{4,1,3,2,0:T(2,128)(2,1)S(1)} copy(bf16[8,2,2,12,4096]{4,2,3,1,0:T(2,128)(2,1)} %bitcast.12) | data formatting | bytes 6291456 | tf_op jit(solution)/shard_map/all_to_all | solution.py:36
  267.9 0.7 constant_dynamic-slice_fusion.4
  268.6 1.0 reshape.85
  269.6 1.1 fusion.5
  270.7 0.3 copy-done.3
  271.0 2.7 fusion.3
  273.7 3.7 %copy.25 = f32[4,2,12,64,64]{4,3,1,2,0:T(8,128)} copy(f32[4,2,12,64,64]{3,4,0,1,2:T(8,128)} %fusion.3) | data formatting | bytes 3145728 | tf_op jit(solution)/shard_map/mul | solution.py:51
  277.4 4.2 %reshape.71 = f32[4,2,12,4096]{3,1,2,0:T(2,128)} reshape(f32[4,2,12,64,64]{4,3,1,2,0:T(8,128)} %copy.25) | data formatting | bytes 3145728 | tf_op jit(solution)/shard_map/reshape | solution.py:52
  (12 shorter events, 0.0 us)
Async XLA Ops:
  6.5 3.7 %copy-start = (bf16[4,2,47,4096]{3,1,2,0:T(2,128)(2,1)S(1)}, bf16[4,2,47,4096]{3,1,2,0:T(2,128)(2,1)}, u32[]{:S(2)}) copy-start(bf16[4,2,47,4096]{3,1,2,0:T(2,128)(2,1)} %param.5) | copy-start | bytes 9240580
  6.5 107.3 %all-gather.3.cloned.1.call-start = ((), (), s32[]{:S(2)}) async-start(), calls=%async_computation.2 | async-start | bytes 7077888 | tf_op jit(solution)/shard_map/all_gather | solution.py:24
  25.4 6.4 %copy-start.4 = (s32[4]{0:T(128)S(1)}, s32[4]{0:T(128)}, u32[]{:S(2)}) copy-start(s32[4]{0:T(128)} %param.7) | copy-start | bytes 52
  25.4 77.3 %all-to-all-start = ((bf16[4,2,4,12,4096]{4,1,3,0,2:T(2,128)(2,1)}), bf16[4,2,4,12,4096]{4,1,3,0,2:T(2,128)(2,1)}, u32[]{:S(2)}, u32[]{:S(2)}) async-start(bf16[4,2,4,12,4096]{4,1,3,0,2:T(2,128)(2,1)} %broadcast_select_fusion), calls=%async_computation | async-start | bytes 6291456 | tf_op jit(solution)/shard_map/all_to_all | solution.py:22
  31.9 188.6 %all-gather.5.cloned.1.call-start = ((), (), s32[]{:S(2)}) async-start(), calls=%async_computation.3 | async-start | bytes 3932160 | tf_op jit(solution)/shard_map/all_gather | solution.py:35
  152.2 5.6 %copy-start.2 = (bf16[4,2,12,64,64]{3,4,0,1,2:T(8,128)(2,1)}, bf16[4,2,12,64,64]{3,4,0,1,2:T(8,128)(2,1)S(1)}, u32[]{:S(2)}) copy-start(bf16[4,2,12,64,64]{3,4,0,1,2:T(8,128)(2,1)S(1)} %fusion.11) | copy-start | bytes 2359300
  220.4 42.3 %all-to-all-start.1 = ((bf16[16,2,12,4096]{3,1,2,0:T(2,128)(2,1)}), bf16[16,2,12,4096]{3,1,2,0:T(2,128)(2,1)}, u32[]{:S(2)}, u32[]{:S(2)}) async-start(bf16[16,2,12,4096]{3,1,2,0:T(2,128)(2,1)} %all-gather.5.cloned.1.call-done), calls=%async_computation.1 | async-start | bytes 6291456 | tf_op jit(solution)/shard_map/all_to_all | solution.py:36
  269.6 1.4 copy-start.3
  273.7 7.9 %copy-start.1 = (bf16[4,2,47,4096]{3,1,2,0:T(2,128)(2,1)S(1)}, bf16[4,2,47,4096]{3,1,2,0:T(2,128)(2,1)}, u32[]{:S(2)}) copy-start(bf16[4,2,47,4096]{3,1,2,0:T(2,128)(2,1)} %param.5) | copy-start | bytes 9240580
Sparse Core Ops, SparseCore 0:
  9.5 48.1 all-gather.2
  157.9 62.5 all-gather.4
where the time goes:
time: 290 us; the launch traced here: 288 us
  waiting for transfers between devices  170 us (59%)
  local copies, waits for them, and re-layouts  71.7 us (25%)
  between operations  13.5 us (5%)
  matrix products  12.2 us (4%)
  starting transfers between devices  11.1 us (4%)
  other arithmetic  10 us (3%)
    all_to_all x1, waiting for transfers between devices, on_device(): lax.all_to_all(packed, 'row', split_axis=2, concat_axis=0, tiled=True)  69.6 us
    all_gather x1, waiting for transfers between devices, on_device(): residual_strip = lax.all_gather(cycle, 'row', axis=0, tiled=True)  62.7 us
    all_to_all x1, waiting for transfers between devices, on_device(): lax.all_to_all(residual_strip, 'col', split_axis=0, concat_axis=1, tiled=...  37.6 us
    reshape x1, local copies, waits for them, and re-layouts, on_device(): piece.reshape(occ_row, piece_count, slot_count, tile_width, tile_width)  17.9 us
    another operation x1, local copies, waits for them, and re-layouts, on_device(): received.reshape(piece_count, occ_col, slot_count, tile_width, tile_width)  11.1 us
    dot_general x1, matrix products, on_device(): jnp.einsum('iksac,kjscb->ijsab', left_tiles, right_tiles, preferred_eleme...  11.1 us
    all_gather x1, local copies, waits for them, and re-layouts, on_device(): piece = lax.all_gather(amplitudes, 'col', axis=1, tiled=True)  9.35 us
    gather x1, local copies, waits for them, and re-layouts, on_device(): packed = jnp.take(integrals, tile_second.reshape(-1), axis=2)  8.51 us
  transfers between devices with their start and end apart: 4, of which 3 were waited for; matrix products, arithmetic and copies ran while one was open for 10% of the time, Pallas kernels for 0%

commit v1 on v0

--- a/solution.py
+++ b/solution.py
@@ -4,6 +4,10 @@
 from jax.sharding import PartitionSpec as P
 
 TILE = 64
+_change_sections = lambda obj, ax_name: jnp.concatenate(
+    jax.lax.all_to_all(jnp.stack(jnp.split(obj, jax.lax.axis_size(ax_name), 2), 0), ax_name, 0, 0),
+    0,
+)
 
 
 def on_device(amplitudes, integrals, pair_lists, tile_counts):
@@ -19,7 +23,7 @@
     tile_second = pair_lists[:, :, 1]
     packed = jnp.take(integrals, tile_second.reshape(-1), axis=2)
     packed = packed.reshape(occ_row, occ_col, row_devices, slot_count, square)
-    received = lax.all_to_all(packed, "row", split_axis=2, concat_axis=0, tiled=True)
+    received = _change_sections(packed, "row")
     received = received.reshape(occ_row * row_devices, occ_col, slot_count, square)
     piece = lax.all_gather(amplitudes, "col", axis=1, tiled=True)
     piece_count = piece.shape[1]

time: 290 us -> 301 us (1.038)
  local copies, waits for them, and re-layouts: 71.7 us -> 79.8 us
    another operation x0 -> x1, other arithmetic: none -> 6.62 us  [jnp.stack(jnp.split(obj, jax.lax.axis_size(ax_name), 2), 0)]
    gather x1 -> x2, local copies, waits for them, and re-layouts: 8.51 us -> 13.8 us  [on_device(): packed = jnp.take(integrals, tile_second.reshape(-1), axis=2)]
    select_n x2, other arithmetic: 6.69 us -> 2.91 us  [on_device(): packed = jnp.take(integrals, tile_second.reshape(-1), axis=2)]
  transfers between devices with their start and end apart: 4 -> 4, of which waited for: 3 -> 3; matrix products, arithmetic and copies ran while one was open for 10% -> 13% of each run, Pallas kernels for 0% -> 0%
where the time goes in v1:
time: 301 us; the launch traced here: 299 us
  waiting for transfers between devices  170 us (56%)
  local copies, waits for them, and re-layouts  79.8 us (27%)
  between operations  13.5 us (4%)
  other arithmetic  12.9 us (4%)
  matrix products  12.2 us (4%)
  starting transfers between devices  11.1 us (4%)
    all_to_all x1, waiting for transfers between devices, jax.lax.all_to_all(jnp.stack(jnp.split(obj, jax.lax.axis_size(ax_name), 2...  69.5 us
    all_gather x1, waiting for transfers between devices, on_device(): residual_strip = lax.all_gather(cycle, 'row', axis=0, tiled=True)  62.7 us
    all_to_all x1, waiting for transfers between devices, on_device(): lax.all_to_all(residual_strip, 'col', split_axis=0, concat_axis=1, tiled=...  37.6 us
    reshape x1, local copies, waits for them, and re-layouts, on_device(): piece.reshape(occ_row, piece_count, slot_count, tile_width, tile_width)  17.9 us
    gather x2, local copies, waits for them, and re-layouts, on_device(): packed = jnp.take(integrals, tile_second.reshape(-1), axis=2)  13.8 us
    dot_general x1, matrix products, on_device(): jnp.einsum('iksac,kjscb->ijsab', left_tiles, right_tiles, preferred_eleme...  11.1 us
    another operation x1, local copies, waits for them, and re-layouts, on_device(): received.reshape(piece_count, occ_col, slot_count, tile_width, tile_width)  11.1 us
    all_gather x1, local copies, waits for them, and re-layouts, on_device(): piece = lax.all_gather(amplitudes, 'col', axis=1, tiled=True)  9.35 us
  transfers between devices with their start and end apart: 4, of which 3 were waited for; matrix products, arithmetic and copies ran while one was open for 13% of the time, Pallas kernels for 0%

profile of v1, /device:TPU:0, one launch (start us, length us, event | category | flops | bytes accessed | tf_op | source)
XLA Modules:
  0.0 299.3 jit_solution(5662175506649471996)
XLA Ops:
  6.5 2.8 copy.32
  9.3 0.0 all-gather.3.cloned.1.call-update
  9.3 0.8 fusion.29
  10.1 0.1 reshape_squeeze.6
  10.2 8.5 %gather_fusion = bf16[48,4,2,4096]{3,2,1,0:T(2,128)(2,1)} fusion(bf16[4,2,47,4096]{3,1,2,0:T(2,128)(2,1)S(1)} %copy-done, s32[1024]{0:T(1024)S(1)} %pad_clamp_fusion), kind=kCustom, calls=%fused_computation | custom fusion | bytes 6291648 | tf_op jit(solution)/shard_map/jit(_take)/gather | solution.py:24
  18.7 5.2 %copy.28 = bf16[4,2,48,4096]{3,1,2,0:T(2,128)(2,1)S(1)} copy(bf16[4,2,48,4096]{3,1,0,2:T(2,128)(2,1)} %bitcast.78) | data formatting | bytes 6291456 | tf_op jit(solution)/shard_map/jit(_take)/gather | solution.py:24
  24.0 2.9 broadcast_select_fusion
  26.9 2.8 slice_bitcast_fusion.3
  29.8 6.6 %pad_maximum_fusion = bf16[4,4,2,1,12,4096]{5,2,4,1,3,0:T(2,128)(2,1)} fusion(bf16[1,4,2,1,12,4096]{5,2,4,1,3,0:T(2,128)(2,1)S(1)} %get-tuple-element.7, bf16[1,4,2,1,12,4096]{5,2,4,1,3,0:T(2,128)(2,1)S(1)} %get-tuple-element.8, bf16[1,4,2,1,12,4096]{5,2,4,1,3,0:T(2,128)(2,1)S(1)} %get-tuple-element.6, bf16[1,4,2,1,12,4096]{5,2,4,1,3,0:T(2,128)(2,1)S(1)} %get-tuple-element.5), kind=kLoop, calls=%fused_computation.5 | loop fusion | flops 4718592 | bytes 6291456 | tf_op jit(solution)/shard_map/stack | solution.py:8
  36.4 6.4 %all-to-all-start = ((bf16[4,4,2,1,12,4096]{5,2,4,1,3,0:T(2,128)(2,1)}), bf16[4,4,2,1,12,4096]{5,2,4,1,3,0:T(2,128)(2,1)}, u32[]{:S(2)}, u32[]{:S(2)}) async-start(bf16[4,4,2,1,12,4096]{5,2,4,1,3,0:T(2,128)(2,1)} %pad_maximum_fusion), calls=%async_computation | async-start | bytes 6291456 | tf_op jit(solution)/shard_map/all_to_all | solution.py:8
  42.8 0.0 all-gather.5.cloned.1.call-start
  42.8 0.7 dynamic_slice.20
  43.5 0.7 compare_convert_fusion
  44.2 69.5 %all-to-all-done = bf16[4,4,2,1,12,4096]{5,2,4,1,3,0:T(2,128)(2,1)} async-done(((bf16[4,4,2,1,12,4096]{5,2,4,1,3,0:T(2,128)(2,1)}), bf16[4,4,2,1,12,4096]{5,2,4,1,3,0:T(2,128)(2,1)}, u32[]{:S(2)}, u32[]{:S(2)}) %all-to-all-start) | async-done | bytes 3145760 | tf_op jit(solution)/shard_map/all_to_all | solution.py:8
  113.7 11.1 %reshape_reshape_reshape.3 = bf16[16,2,12,64,64]{4,3,1,2,0:T(8,128)(2,1)} reshape(bf16[4,4,2,1,12,4096]{5,2,4,1,3,0:T(2,128)(2,1)} %all-to-all-done) | data formatting | bytes 6291456 | tf_op jit(solution)/shard_map/reshape;reshape;reshape | solution.py:31
  124.7 9.3 %copy.33 = bf16[4,16,12,4096]{3,1,0,2:T(8,128)(2,1)} copy(bf16[4,16,12,4096]{3,0,2,1:T(4,128)(2,1)} %all-gather.3.cloned.1.call-done) | data formatting | bytes 12582912 | tf_op jit(solution)/shard_map/all_gather | solution.py:28
  134.1 17.9 %reshape.80 = bf16[4,16,12,64,64,1]{4,3,1,0,2,5:T(8,128)(2,1)} reshape(bf16[4,16,12,4096]{3,1,0,2:T(8,128)(2,1)} %copy.33) | data formatting | bytes 12582912 | tf_op jit(solution)/shard_map/reshape | solution.py:30
  152.0 11.1 %fusion.11 = bf16[4,2,12,64,64]{3,4,0,1,2:T(8,128)(2,1)S(1)} fusion(f32[12]{0:T(128)S(1)} %compare_convert_fusion, bf16[4,16,12,64,64,1]{4,3,1,0,2,5:T(8,128)(2,1)} %reshape.80, bf16[16,2,12,64,64]{4,3,1,2,0:T(8,128)(2,1)} %reshape_reshape_reshape.3), kind=kOutput, calls=%fused_computation.12 | convolution fusion | flops 806092800 | bytes 10223664 | tf_op jit(solution)/shard_map/iksac,kjscb->ijsab/dot_general | solution.py:32
  163.1 1.7 copy.35
  164.8 3.8 %reshape.68 = bf16[4,2,12,4096]{3,1,2,0:T(2,128)(2,1)} reshape(bf16[4,2,12,64,64]{4,3,1,2,0:T(8,128)(2,1)} %copy.35) | data formatting | bytes 1572864 | tf_op jit(solution)/shard_map/reshape | solution.py:38
  168.6 0.0 all-gather.5.cloned.1.call-update
  168.7 62.7 %all-gather.5.cloned.1.call-done = bf16[16,2,12,4096]{3,1,2,0:T(2,128)(2,1)} async-done(((bf16[4,2,12,4096]{3,1,2,0:T(2,128)(2,1)}), bf16[16,2,12,4096]{3,1,2,0:T(2,128)(2,1)}) %all-gather.5.cloned.1.call-update) | async-done | bytes 3145744 | tf_op jit(solution)/shard_map/all_gather | solution.py:39
  231.3 4.7 %all-to-all-start.1 = ((bf16[16,2,12,4096]{3,1,2,0:T(2,128)(2,1)}), bf16[16,2,12,4096]{3,1,2,0:T(2,128)(2,1)}, u32[]{:S(2)}, u32[]{:S(2)}) async-start(bf16[16,2,12,4096]{3,1,2,0:T(2,128)(2,1)} %all-gather.5.cloned.1.call-done), calls=%async_computation.1 | async-start | bytes 6291456 | tf_op jit(solution)/shard_map/all_to_all | solution.py:40
  236.0 37.6 %all-to-all-done.1 = bf16[16,2,12,4096]{3,1,2,0:T(2,128)(2,1)} async-done(((bf16[16,2,12,4096]{3,1,2,0:T(2,128)(2,1)}), bf16[16,2,12,4096]{3,1,2,0:T(2,128)(2,1)}, u32[]{:S(2)}, u32[]{:S(2)}) %all-to-all-start.1) | async-done | bytes 3145760 | tf_op jit(solution)/shard_map/all_to_all | solution.py:40
  273.6 5.1 %copy.36 = bf16[8,2,2,12,4096]{4,1,3,2,0:T(2,128)(2,1)S(1)} copy(bf16[8,2,2,12,4096]{4,2,3,1,0:T(2,128)(2,1)} %bitcast.14) | data formatting | bytes 6291456 | tf_op jit(solution)/shard_map/all_to_all | solution.py:40
  278.8 0.7 constant_dynamic-slice_fusion.4
  279.4 1.0 reshape.84
  280.5 1.1 fusion.5
  281.6 0.3 copy-done.3
  281.9 2.7 fusion.3
  284.6 3.7 %copy.40 = f32[4,2,12,64,64]{4,3,1,2,0:T(8,128)} copy(f32[4,2,12,64,64]{3,4,0,1,2:T(8,128)} %fusion.3) | data formatting | bytes 3145728 | tf_op jit(solution)/shard_map/mul | solution.py:55
  288.3 4.2 %reshape.70 = f32[4,2,12,4096]{3,1,2,0:T(2,128)} reshape(f32[4,2,12,64,64]{4,3,1,2,0:T(8,128)} %copy.40) | data formatting | bytes 3145728 | tf_op jit(solution)/shard_map/reshape | solution.py:56
  (15 shorter events, 0.1 us)
Async XLA Ops:
  6.5 3.7 %copy-start = (bf16[4,2,47,4096]{3,1,2,0:T(2,128)(2,1)S(1)}, bf16[4,2,47,4096]{3,1,2,0:T(2,128)(2,1)}, u32[]{:S(2)}) copy-start(bf16[4,2,47,4096]{3,1,2,0:T(2,128)(2,1)} %param.5) | copy-start | bytes 9240580
  6.5 118.2 %all-gather.3.cloned.1.call-start = ((), (), s32[]{:S(2)}) async-start(), calls=%async_computation.2 | async-start | bytes 7077888 | tf_op jit(solution)/shard_map/all_gather | solution.py:28
  36.4 6.4 %copy-start.4 = (s32[4]{0:T(128)S(1)}, s32[4]{0:T(128)}, u32[]{:S(2)}) copy-start(s32[4]{0:T(128)} %param.7) | copy-start | bytes 52
  36.4 77.3 %all-to-all-start = ((bf16[4,4,2,1,12,4096]{5,2,4,1,3,0:T(2,128)(2,1)}), bf16[4,4,2,1,12,4096]{5,2,4,1,3,0:T(2,128)(2,1)}, u32[]{:S(2)}, u32[]{:S(2)}) async-start(bf16[4,4,2,1,12,4096]{5,2,4,1,3,0:T(2,128)(2,1)} %pad_maximum_fusion), calls=%async_computation | async-start | bytes 6291456 | tf_op jit(solution)/shard_map/all_to_all | solution.py:8
  42.8 188.5 %all-gather.5.cloned.1.call-start = ((), (), s32[]{:S(2)}) async-start(), calls=%async_computation.3 | async-start | bytes 3932160 | tf_op jit(solution)/shard_map/all_gather | solution.py:39
  163.1 5.5 %copy-start.2 = (bf16[4,2,12,64,64]{3,4,0,1,2:T(8,128)(2,1)}, bf16[4,2,12,64,64]{3,4,0,1,2:T(8,128)(2,1)S(1)}, u32[]{:S(2)}) copy-start(bf16[4,2,12,64,64]{3,4,0,1,2:T(8,128)(2,1)S(1)} %fusion.11) | copy-start | bytes 2359300
  231.3 42.3 %all-to-all-start.1 = ((bf16[16,2,12,4096]{3,1,2,0:T(2,128)(2,1)}), bf16[16,2,12,4096]{3,1,2,0:T(2,128)(2,1)}, u32[]{:S(2)}, u32[]{:S(2)}) async-start(bf16[16,2,12,4096]{3,1,2,0:T(2,128)(2,1)} %all-gather.5.cloned.1.call-done), calls=%async_computation.1 | async-start | bytes 6291456 | tf_op jit(solution)/shard_map/all_to_all | solution.py:40
  280.5 1.4 copy-start.3
  284.6 7.9 %copy-start.1 = (bf16[4,2,47,4096]{3,1,2,0:T(2,128)(2,1)S(1)}, bf16[4,2,47,4096]{3,1,2,0:T(2,128)(2,1)}, u32[]{:S(2)}) copy-start(bf16[4,2,47,4096]{3,1,2,0:T(2,128)(2,1)} %param.5) | copy-start | bytes 9240580
Sparse Core Ops, SparseCore 0:
  9.5 48.1 all-gather.2
  168.8 62.4 all-gather.4
